TPU v7x, 32 devices: a whole 2x2x4 slice. The times are simulated.
32 devices in a mesh: nodes: 8 (over y, x, core), heads: 4 (over z).
Axes of the slice: x: 2, y: 2, z: 4, core: 2. Of those that a mesh axis runs over, the one named last changes fastest.
Arguments:
- grid_state: bfloat16 [8192, 1024], P('nodes', 'heads'), may hold values from -6 to 6
- mesh_state: bfloat16 [2048, 1024], P('nodes', 'heads'), may hold values from -6 to 6
- encoder_query: bfloat16 [1024, 512], P('nodes', 'heads'), may hold values from -0.1875 to 0.1875
- encoder_key: bfloat16 [1024, 512], P('nodes', 'heads'), may hold values from -0.1875 to 0.1875
- encoder_value: bfloat16 [1024, 512], P('nodes', 'heads'), may hold values from -0.1875 to 0.1875
- encoder_output: bfloat16 [512, 1024], P('heads', 'nodes'), may hold values from -0.25 to 0.25
- window_query: bfloat16 [1024, 512], P('nodes', 'heads'), may hold values from -0.1875 to 0.1875
- window_key: bfloat16 [1024, 512], P('nodes', 'heads'), may hold values from -0.1875 to 0.1875
- window_value: bfloat16 [1024, 512], P('nodes', 'heads'), may hold values from -0.1875 to 0.1875
- window_output: bfloat16 [512, 1024], P('heads', 'nodes'), may hold values from -0.25 to 0.25
- expand_weight: bfloat16 [1024, 2048], P('nodes', 'heads'), may hold values from -0.1875 to 0.1875
- shrink_weight: bfloat16 [2048, 1024], P('heads', 'nodes'), may hold values from -0.125 to 0.125
- decoder_query: bfloat16 [1024, 512], P('nodes', 'heads'), may hold values from -0.1875 to 0.1875
- decoder_key: bfloat16 [1024, 512], P('nodes', 'heads'), may hold values from -0.1875 to 0.1875
- decoder_value: bfloat16 [1024, 512], P('nodes', 'heads'), may hold values from -0.1875 to 0.1875
- decoder_output: bfloat16 [512, 1024], P('heads', 'nodes'), may hold values from -0.25 to 0.25
- encoder_blocks: int32 [16, 8], P('nodes'), may hold values from 0 to 63, as said below
- encoder_count: int32 [16], P('nodes'), may hold values from 2 to 8, as said below
- window_offsets: int32 [16, 4], P('nodes'), may hold values from -2 to 2, as said below
- decoder_blocks: int32 [64, 3], P('nodes'), may hold values from 0 to 15, as said below
- decoder_count: int32 [64], P('nodes'), may hold values from 1 to 3, as said below
Outputs:
- grid_out: bfloat16 [8192, 1024], P('nodes', 'heads')
- mesh_out: bfloat16 [2048, 1024], P('nodes', 'heads')
Inputs may be any that keep to these rules, and one draw needn't show every extreme that they name: `encoder_blocks`: row m names 8 different grid blocks; each lies among the grid blocks of the index of nodes that holds mesh block m, or in the nearer half of the grid blocks of the index on either side. The first encoder_count[m] slots of row m are live; every mesh block held by the first or last eighth of the indices of nodes has all 8 slots live. `window_offsets`: each row holds 4 different offsets, the first of them 0. `decoder_blocks`: row g names 3 different mesh blocks; each lies among the mesh blocks of the index of nodes that holds grid block g, or is the one block next to them on either side. The first decoder_count[g] slots of row g are live; every grid block of the first index of nodes has all 3 slots live.
All inputs are finite; a program needn't handle non-finite values.
Results may differ from a plain program's by a relative error of at most 0.012.
Values may be sent and summed in bfloat16 or wider, within the bound.
A program may use at most 64 MiB of HBM per device.

v0:
```python
import math
import jax
import jax.numpy as jnp
from jax import lax
from jax.sharding import PartitionSpec as P

HEAD_DIM = 64
TILE = 128
EPSILON = 1e-05


def with_halo(x, sides, width):
    for axis, dim in sides:
        size, length = (lax.axis_size(axis), x.shape[dim])
        up = [(i, (i + 1) % size) for i in range(size - 1)]
        down = [(j, i) for i, j in up]
        last = lax.slice_in_dim(x, length - width, length, axis=dim)
        first = lax.slice_in_dim(x, 0, width, axis=dim)
        before = lax.ppermute(last, axis, up)
        after = lax.ppermute(first, axis, down)
        x = jnp.concatenate([before, x, after], axis=dim)
    return x


def normalize(values):
    values = values.astype(jnp.float32)
    average = jnp.mean(values, axis=-1, keepdims=True)
    centred = values - average
    spread = jnp.mean(centred * centred, axis=-1, keepdims=True)
    return (centred * lax.rsqrt(spread + EPSILON)).astype(jnp.bfloat16)


def add_terms(source, totals, pieces):
    result = []
    for running, weight_piece in zip(totals, pieces):
        result.append(jnp.dot(source, weight_piece, preferred_element_type=jnp.float32))
    return tuple(result)


def column_terms(source, weight_piece):
    return jnp.dot(source, weight_piece, preferred_element_type=jnp.float32)


def attend(queries, key_rows, value_rows, key_mask):
    batch_size, row_count, column_count = queries.shape
    head_count = column_count // HEAD_DIM
    split_query = queries.reshape(batch_size, row_count, head_count, HEAD_DIM)
    split_key = key_rows.reshape(batch_size, key_rows.shape[1], head_count, HEAD_DIM)
    split_value = value_rows.reshape(batch_size, value_rows.shape[1], head_count, HEAD_DIM)
    scores = jnp.einsum(
        "bqhd,bkhd->bhqk", split_query, split_key, preferred_element_type=jnp.float32
    )
    scores = jnp.where(key_mask[:, None, None, :], scores, -1e30)
    highest = jnp.max(scores, axis=-1, keepdims=True)
    weights = jnp.exp(scores - highest)
    weights = (weights / jnp.sum(weights, axis=-1, keepdims=True)).astype(jnp.bfloat16)
    mixture = jnp.einsum(
        "bhqk,bkhd->bqhd", weights, split_value, preferred_element_type=jnp.float32
    )
    return mixture.reshape(batch_size, row_count, column_count).astype(jnp.bfloat16)


def attend_blocks(queries, key_rows, value_rows, key_mask):
    tile_count = queries.shape[0]
    group_size = math.gcd(tile_count, 4)

    def one_group(arguments):
        return attend(arguments[0], arguments[1], arguments[2], arguments[3])

    grouped = tuple(
        (
            member.reshape((tile_count // group_size, group_size) + member.shape[1:])
            for member in (queries, key_rows, value_rows, key_mask)
        )
    )
    return lax.map(one_group, grouped).reshape(queries.shape)


def pick_tiles(stacked, tile_count, chosen):
    column_count = stacked.shape[-1]
    tile_view = stacked.reshape(2, tile_count, TILE, column_count)
    picked = jnp.take(tile_view, chosen, axis=1)
    shaped = picked.reshape(2, chosen.shape[0], chosen.shape[1] * TILE, column_count)
    return (shaped[0], shaped[1])


def slot_mask(live_count, slot_total):
    live = jnp.arange(slot_total, dtype=jnp.int32)[None, :] < live_count[:, None]
    return jnp.repeat(live, TILE, axis=1)


def local(
    grid_state,
    mesh_state,
    encoder_query,
    encoder_key,
    encoder_value,
    encoder_output,
    window_query,
    window_key,
    window_value,
    window_output,
    expand_weight,
    shrink_weight,
    decoder_query,
    decoder_key,
    decoder_value,
    decoder_output,
    encoder_blocks,
    encoder_count,
    window_offsets,
    decoder_blocks,
    decoder_count,
):
    scaling = HEAD_DIM ** (-0.5)
    position = lax.axis_index("nodes")
    head_lane = lax.axis_index("heads")
    grid_rows = grid_state.shape[0]
    mesh_rows = mesh_state.shape[0]
    feature_count = mesh_state.shape[1]
    grid_tiles = grid_rows // TILE
    mesh_tiles = mesh_rows // TILE
    all_mesh_tiles = mesh_tiles * lax.axis_size("nodes")
    head_columns = encoder_key.shape[1]
    grid_blank = jnp.zeros((grid_rows, head_columns), jnp.float32)
    mesh_blank = jnp.zeros((mesh_rows, head_columns), jnp.float32)
    grid_full = lax.all_gather(grid_state, "heads", axis=1, tiled=True)
    grid_norm = normalize(grid_full)
    grid_key, grid_value, grid_query = add_terms(
        grid_norm,
        (grid_blank, grid_blank, grid_blank),
        (
            lax.all_gather(encoder_key, "nodes", axis=0, tiled=True),
            lax.all_gather(encoder_value, "nodes", axis=0, tiled=True),
            lax.all_gather(decoder_query, "nodes", axis=0, tiled=True),
        ),
    )
    grid_queries = (grid_query * scaling).astype(jnp.bfloat16)
    mesh_full = lax.all_gather(mesh_state, "heads", axis=1, tiled=True)
    mesh_norm = normalize(mesh_full)
    (mesh_query,) = add_terms(
        mesh_norm, (mesh_blank,), (lax.all_gather(encoder_query, "nodes", axis=0, tiled=True),)
    )
    mesh_queries = (mesh_query * scaling).astype(jnp.bfloat16)
    rim_tiles = grid_tiles // 2
    stacked = jnp.stack([grid_key.astype(jnp.bfloat16), grid_value.astype(jnp.bfloat16)])
    padded = with_halo(stacked, (("nodes", 1),), rim_tiles * TILE)
    local_index = encoder_blocks - (position * grid_tiles - rim_tiles)
    key_rows, value_rows = pick_tiles(padded, grid_tiles + 2 * rim_tiles, local_index)
    key_mask = slot_mask(encoder_count, encoder_blocks.shape[1])
    encoded = attend_blocks(
        mesh_queries.reshape(mesh_tiles, TILE, head_columns), key_rows, value_rows, key_mask
    ).reshape(mesh_rows, head_columns)
    encoder_terms = column_terms(
        encoded, lax.all_gather(encoder_output, "nodes", axis=1, tiled=True)
    )
    encoder_sum = lax.psum(encoder_terms.astype(jnp.bfloat16), "heads").astype(jnp.float32)
    mesh_one = (mesh_full.astype(jnp.float32) + encoder_sum).astype(jnp.bfloat16)
    norm_one = normalize(mesh_one)
    window_queries, window_keys, window_values = add_terms(
        norm_one,
        (mesh_blank, mesh_blank, mesh_blank),
        (
            lax.all_gather(window_query, "nodes", axis=0, tiled=True),
            lax.all_gather(window_key, "nodes", axis=0, tiled=True),
            lax.all_gather(window_value, "nodes", axis=0, tiled=True),
        ),
    )
    window_queries = (window_queries * scaling).astype(jnp.bfloat16)
    stacked = jnp.stack([window_keys.astype(jnp.bfloat16), window_values.astype(jnp.bfloat16)])
    padded = with_halo(stacked, (("nodes", 1),), mesh_rows)
    tile_here = jnp.arange(mesh_tiles, dtype=jnp.int32)[:, None]
    key_rows, value_rows = pick_tiles(
        padded, 3 * mesh_tiles, tile_here + mesh_tiles + window_offsets
    )
    reached = position * mesh_tiles + tile_here + window_offsets
    key_mask = jnp.repeat((reached >= 0) & (reached < all_mesh_tiles), TILE, axis=1)
    windowed = attend_blocks(
        window_queries.reshape(mesh_tiles, TILE, head_columns), key_rows, value_rows, key_mask
    ).reshape(mesh_rows, head_columns)
    window_terms = column_terms(
        windowed, lax.all_gather(window_output, "nodes", axis=1, tiled=True)
    )
    window_sum = lax.psum(window_terms.astype(jnp.bfloat16), "heads").astype(jnp.float32)
    mesh_two = (mesh_one.astype(jnp.float32) + window_sum).astype(jnp.bfloat16)
    norm_two = normalize(mesh_two)
    hidden_blank = jnp.zeros((mesh_rows, expand_weight.shape[1]), jnp.float32)
    (hidden,) = add_terms(
        norm_two, (hidden_blank,), (lax.all_gather(expand_weight, "nodes", axis=0, tiled=True),)
    )
    hidden = jax.nn.gelu(hidden, approximate=False).astype(jnp.bfloat16)
    hidden_terms = column_terms(hidden, lax.all_gather(shrink_weight, "nodes", axis=1, tiled=True))
    hidden_sum = lax.psum(hidden_terms.astype(jnp.bfloat16), "heads").astype(jnp.float32)
    mesh_three = (mesh_two.astype(jnp.float32) + hidden_sum).astype(jnp.bfloat16)
    mesh_out = lax.dynamic_slice_in_dim(mesh_three, head_lane * feature_count, feature_count, 1)
    norm_three = normalize(mesh_three)
    mesh_keys, mesh_values = add_terms(
        norm_three,
        (mesh_blank, mesh_blank),
        (
            lax.all_gather(decoder_key, "nodes", axis=0, tiled=True),
            lax.all_gather(decoder_value, "nodes", axis=0, tiled=True),
        ),
    )
    stacked = jnp.stack([mesh_keys.astype(jnp.bfloat16), mesh_values.astype(jnp.bfloat16)])
    padded = with_halo(stacked, (("nodes", 1),), TILE)
    local_index = decoder_blocks - (position * mesh_tiles - 1)
    key_rows, value_rows = pick_tiles(padded, mesh_tiles + 2, local_index)
    key_mask = slot_mask(decoder_count, decoder_blocks.shape[1])
    decoded = attend_blocks(
        grid_queries.reshape(grid_tiles, TILE, head_columns), key_rows, value_rows, key_mask
    ).reshape(grid_rows, head_columns)
    quarter = lax.all_to_all(decoded, "heads", split_axis=0, concat_axis=1, tiled=True)
    whole_output = lax.all_gather(decoder_output, "heads", axis=0, tiled=True)
    decoder_terms = column_terms(quarter, lax.all_gather(whole_output, "nodes", axis=1, tiled=True))
    quarter_rows = quarter.shape[0]
    base_rows = lax.dynamic_slice_in_dim(grid_full, head_lane * quarter_rows, quarter_rows, 0)
    updated = (base_rows.astype(jnp.float32) + decoder_terms).astype(jnp.bfloat16)
    grid_out = lax.all_to_all(updated, "heads", split_axis=1, concat_axis=0, tiled=True)
    return (grid_out, mesh_out)


def solution(mesh):
    in_specs = (
        P("nodes", "heads"),
        P("nodes", "heads"),
        P("nodes", "heads"),
        P("nodes", "heads"),
        P("nodes", "heads"),
        P("heads", "nodes"),
        P("nodes", "heads"),
        P("nodes", "heads"),
        P("nodes", "heads"),
        P("heads", "nodes"),
        P("nodes", "heads"),
        P("heads", "nodes"),
        P("nodes", "heads"),
        P("nodes", "heads"),
        P("nodes", "heads"),
        P("heads", "nodes"),
        P("nodes", None),
        P("nodes"),
        P("nodes", None),
        P("nodes", None),
        P("nodes"),
    )
    out_specs = (P("nodes", "heads"), P("nodes", "heads"))
    return jax.shard_map(local, mesh=mesh, in_specs=in_specs, out_specs=out_specs, check_vma=False)
```

profile of v0, /device:TPU:0, one launch (start us, length us, event | category | flops | bytes accessed | tf_op | source)
XLA Modules:
  0.0 340.2 jit_solution(1236470662287655279)
XLA Ops:
  8.8 11.0 %all_gather.53 = bf16[1024,128]{1,0:T(8,128)(2,1)S(1)} all-gather(bf16[128,128]{1,0:T(8,128)(2,1)} %param.26), channel_id=1, replica_groups=mesh['nodes'=8,'heads'=4] {'nodes'}, dimensions={0}, use_global_device_ids=true | all-gather | bytes 294912 | tf_op jit(solution)/shard_map/all_gather | solution.py:133
  19.8 9.0 %all_gather.54 = bf16[1024,128]{1,0:T(8,128)(2,1)S(1)} all-gather(bf16[128,128]{1,0:T(8,128)(2,1)} %param.27), channel_id=1, replica_groups=mesh['nodes'=8,'heads'=4] {'nodes'}, dimensions={0}, use_global_device_ids=true | all-gather | bytes 294912 | tf_op jit(solution)/shard_map/all_gather | solution.py:134
  28.9 8.5 %all_gather.55 = bf16[1024,128]{1,0:T(8,128)(2,1)S(1)} all-gather(bf16[128,128]{1,0:T(8,128)(2,1)} %param.25), channel_id=1, replica_groups=mesh['nodes'=8,'heads'=4] {'nodes'}, dimensions={0}, use_global_device_ids=true | all-gather | bytes 294912 | tf_op jit(solution)/shard_map/all_gather | solution.py:142
  37.4 23.2 %all_gather.52 = bf16[256,1024]{1,0:T(8,128)(2,1)S(1)} all-gather(bf16[256,256]{1,0:T(8,128)(2,1)} %param.24), channel_id=1, replica_groups=mesh['nodes'=8,'heads'=4] {'heads'}, dimensions={1}, use_global_device_ids=true | all-gather | bytes 655360 | tf_op jit(solution)/shard_map/all_gather | solution.py:139
  61.9 1.0 fusion.26
  62.8 4.9 %all-gather.5.cloned.1.call-done = bf16[1024,1024]{1,0:T(8,128)(2,1)} async-done(((bf16[1024,256]{1,0:T(8,128)(2,1)}), bf16[1024,1024]{1,0:T(8,128)(2,1)}) %all-gather.5.cloned.1.call-update) | async-done | bytes 2097168 | tf_op jit(solution)/shard_map/all_gather | solution.py:127
  67.8 2.1 convert_reduce_fusion
  73.5 2.4 collective-permute-start
  75.9 1.3 collective-permute-start.1
  77.9 0.9 reshape.241
  78.8 1.3 reshape.221
  80.1 12.1 %all_gather.56 = bf16[128,1024]{1,0:T(8,128)(2,1)S(1)} all-gather(bf16[128,128]{1,0:T(8,128)(2,1)} %param.28), channel_id=1, replica_groups=mesh['nodes'=8,'heads'=4] {'nodes'}, dimensions={1}, use_global_device_ids=true | all-gather | bytes 294912 | tf_op jit(solution)/shard_map/all_gather | solution.py:155
  92.9 2.1 pad_maximum_fusion
  95.0 2.9 gather_fusion
  97.9 2.4 copy.50
  100.3 1.4 select_bitcast_fusion.1
  102.5 2.1 reshape.205
  104.6 1.0 reshape.203
  105.6 1.8 fusion.171
  107.5 2.8 fusion.28
  110.3 0.9 copy.53
  111.2 1.1 convolution_convert_fusion.3
  112.5 10.1 %all_gather.59 = bf16[1024,128]{1,0:T(8,128)(2,1)} all-gather(bf16[128,128]{1,0:T(8,128)(2,1)} %param.29), channel_id=1, replica_groups=mesh['nodes'=8,'heads'=4] {'nodes'}, dimensions={0}, use_global_device_ids=true | all-gather | bytes 294912 | tf_op jit(solution)/shard_map/all_gather | solution.py:164
  122.6 10.1 %all_gather.57 = bf16[1024,128]{1,0:T(8,128)(2,1)} all-gather(bf16[128,128]{1,0:T(8,128)(2,1)} %param.30), channel_id=1, replica_groups=mesh['nodes'=8,'heads'=4] {'nodes'}, dimensions={0}, use_global_device_ids=true | all-gather | bytes 294912 | tf_op jit(solution)/shard_map/all_gather | solution.py:165
  132.7 9.5 %all_gather.58 = bf16[1024,128]{1,0:T(8,128)(2,1)} all-gather(bf16[128,128]{1,0:T(8,128)(2,1)S(1)} %copy-done.11), channel_id=1, replica_groups=mesh['nodes'=8,'heads'=4] {'nodes'}, dimensions={0}, use_global_device_ids=true | all-gather | bytes 294912 | tf_op jit(solution)/shard_map/all_gather | solution.py:166
  142.2 9.3 %all_gather.60 = bf16[128,1024]{1,0:T(8,128)(2,1)S(1)} all-gather(bf16[128,128]{1,0:T(8,128)(2,1)S(1)} %copy-done.12), channel_id=1, replica_groups=mesh['nodes'=8,'heads'=4] {'nodes'}, dimensions={1}, use_global_device_ids=true | all-gather | bytes 294912 | tf_op jit(solution)/shard_map/all_gather | solution.py:182
  151.6 1.3 convert_reduce_fusion.2
  154.0 2.3 collective-permute-start.2
  156.3 1.3 collective-permute-start.3
  158.7 0.9 collective-permute-done.3
  159.7 1.0 pad_maximum_fusion.1
  160.7 1.4 gather_fusion.1
  162.1 1.3 copy.54
  164.6 1.1 reshape.209
  165.7 1.3 convolution_select_fusion.1
  167.5 2.6 fusion.31
  170.2 1.1 convolution_convert_fusion.2
  172.6 38.8 %all-reduce.6.cloned.1.call-done = bf16[256,1024]{1,0:T(8,128)(2,1)} async-done(((bf16[256,1024]{1,0:T(8,128)(2,1)}), bf16[256,1024]{1,0:T(8,128)(2,1)}) %all-reduce.6.cloned.1.call-update) | async-done | bytes 524304 | tf_op jit(solution)/shard_map/psum | solution.py:184
  211.3 1.3 convert_reduce_fusion.1
  213.0 10.4 %all-gather.9.cloned.1.call-done = bf16[512,1024]{1,0:T(8,128)(2,1)} async-done(((bf16[512,128]{1,0:T(8,128)(2,1)}), bf16[512,1024]{1,0:T(8,128)(2,1)}) %all-gather.9.cloned.1.call-update) | async-done | bytes 1048592 | tf_op jit(solution)/shard_map/all_gather | solution.py:192
  223.4 4.3 %convolution_convert_fusion.1 = bf16[256,1024]{1,0:T(8,128)(2,1)} fusion(bf16[512,1024]{1,0:T(8,128)(2,1)} %all-gather.9.cloned.1.call-done, bf16[1024,512]{1,0:T(8,128)(2,1)} %all-gather.7.cloned.1.call-done, bf16[256,1024]{1,0:T(8,128)(2,1)S(1)} %get-tuple-element.106, f32[256]{0:T(256)S(1)} %add_rsqrt_fusion.2, f32[256]{0:T(256)S(1)} %broadcast_multiply_fusion.2), kind=kOutput, calls=%fused_computation.44 | convolution fusion | flops 546701312 | bytes 3147776 | tf_op jit(solution)/shard_map/dot_general | solution.py:41
  227.8 15.2 %all_gather.66 = bf16[512,128]{1,0:T(8,128)(2,1)} all-gather(bf16[128,128]{1,0:T(8,128)(2,1)S(1)} %copy-done.13), channel_id=1, replica_groups=mesh['nodes'=8,'heads'=4] {'heads'}, dimensions={0}, use_global_device_ids=true | all-gather | bytes 163840 | tf_op jit(solution)/shard_map/all_gather | solution.py:214
  243.0 9.3 %all_gather.64 = bf16[1024,128]{1,0:T(8,128)(2,1)S(1)} all-gather(bf16[128,128]{1,0:T(8,128)(2,1)S(1)} %copy-done.14), channel_id=1, replica_groups=mesh['nodes'=8,'heads'=4] {'nodes'}, dimensions={0}, use_global_device_ids=true | all-gather | bytes 294912 | tf_op jit(solution)/shard_map/all_gather | solution.py:202
  252.2 8.3 %all_gather.63 = bf16[1024,128]{1,0:T(8,128)(2,1)S(1)} all-gather(bf16[128,128]{1,0:T(8,128)(2,1)S(1)} %copy-done.15), channel_id=1, replica_groups=mesh['nodes'=8,'heads'=4] {'nodes'}, dimensions={0}, use_global_device_ids=true | all-gather | bytes 294912 | tf_op jit(solution)/shard_map/all_gather | solution.py:201
  260.9 9.2 %all_gather.65 = bf16[1024,128]{1,0:T(8,128)(2,1)S(1)} all-gather(bf16[128,128]{1,0:T(8,128)(2,1)S(1)} %copy-done.16), channel_id=1, replica_groups=mesh['nodes'=8,'heads'=4] {'nodes'}, dimensions={0}, use_global_device_ids=true | all-gather | bytes 294912 | tf_op jit(solution)/shard_map/all_gather | solution.py:135
  270.3 1.4 convert_reduce_fusion.4
  272.8 2.3 collective-permute-start.4
  275.1 1.5 collective-permute-start.5
  278.2 1.9 gather_fusion.2
  280.2 1.5 copy.59
  281.9 1.3 fusion.168
  283.2 13.0 %while.2 = (s32[]{:T(128)}, bf16[2,4,128,128]{3,2,1,0:T(8,128)(2,1)}, bf16[2,4,384,128]{3,2,1,0:T(8,128)(2,1)}, pred[2,4,384]{2,1,0:T(4,128)(4,1)S(1)}, bf16[2,4...) while((s32[]{:T(128)}, bf16[2,4,128,128]{3,2,1,0:T(8,128)(2,1)}, ...), condition=%wide.region_20.21_spmd, body=%wide.region_17.20_spmd.sunk | while | flops 102695296 | bytes 10498709 | solution.py:76
  283.2 1.2 constant_dynamic-slice_fusion.6
  284.7 1.8 fusion.212
  286.8 2.0 convolution_convert_fusion.13
  289.7 1.2 constant_dynamic-slice_fusion.6
  291.2 1.8 fusion.212
  293.3 2.0 convolution_convert_fusion.13
  296.2 4.6 %all-to-all-start = ((bf16[4,256,128]{2,1,0:T(8,128)(2,1)}), bf16[4,256,128]{2,1,0:T(8,128)(2,1)S(1)}, u32[]{:S(2)}, u32[]{:S(2)}) async-start(bf16[4,256,128]{2,1,0:T(8,128)(2,1)} %bitcast.146), calls=%async_computation | async-start | bytes 524288 | tf_op jit(solution)/shard_map/all_to_all | solution.py:213
  300.8 8.6 %all-to-all-done = bf16[4,256,128]{2,1,0:T(8,128)(2,1)S(1)} async-done(((bf16[4,256,128]{2,1,0:T(8,128)(2,1)}), bf16[4,256,128]{2,1,0:T(8,128)(2,1)S(1)}, u32[]{:S(2)}, u32[]{:S(2)}) %all-to-all-start) | async-done | bytes 262176 | tf_op jit(solution)/shard_map/all_to_all | solution.py:213
  309.6 1.7 fusion.14
  312.1 4.1 %all-to-all-start.1 = ((bf16[256,4,256]{2,0,1:T(8,128)(2,1)}), bf16[256,4,256]{2,0,1:T(8,128)(2,1)S(1)}, u32[]{:S(2)}, u32[]{:S(2)}) async-start(bf16[256,4,256]{2,0,1:T(8,128)(2,1)} %bitcast.110), calls=%async_computation.1 | async-start | bytes 1048576 | tf_op jit(solution)/shard_map/all_to_all | solution.py:219
  316.2 1.6 constant_dynamic-slice_fusion.3
  317.8 14.3 %all-to-all-done.1 = bf16[256,4,256]{2,0,1:T(8,128)(2,1)S(1)} async-done(((bf16[256,4,256]{2,0,1:T(8,128)(2,1)}), bf16[256,4,256]{2,0,1:T(8,128)(2,1)S(1)}, u32[]{:S(2)}, u32[]{:S(2)}) %all-to-all-start.1) | async-done | bytes 524320 | tf_op jit(solution)/shard_map/all_to_all | solution.py:219
  (149 shorter events, 21.7 us)
Async XLA Ops:
  8.0 53.0 %copy-start.22 = (s32[2]{0:T(128)S(1)}, s32[2]{0:T(128)}, u32[]{:S(2)}) copy-start(s32[2]{0:T(128)} %param.40) | copy-start | bytes 28
  8.0 53.2 %copy-start.19 = (s32[2,4]{1,0:T(2,128)S(1)}, s32[2,4]{1,0:T(2,128)}, u32[]{:S(2)}) copy-start(s32[2,4]{1,0:T(2,128)} %param.41) | copy-start | bytes 100
  8.0 59.8 %all-gather.5.cloned.1.call-start = ((), (), s32[]{:S(2)}) async-start(), calls=%async_computation.2 | async-start | bytes 2621440 | tf_op jit(solution)/shard_map/all_gather | solution.py:127
  8.8 142.8 %all-reduce.4.cloned.1.call-start = ((), (), s32[]{:S(2)}) async-start(), calls=%async_computation.3 | async-start | bytes 1048576 | tf_op jit(solution)/shard_map/psum | solution.py:157
  67.8 2.2 copy-start
  71.3 1.4 copy-start.1
  72.0 5.2 %copy-start.18 = (s32[2,8]{1,0:T(2,128)S(1)}, s32[2,8]{1,0:T(2,128)}, u32[]{:S(2)}) copy-start(s32[2,8]{1,0:T(2,128)} %param.39) | copy-start | bytes 196
  73.5 19.3 %collective-permute-start = (bf16[2,512,128]{2,1,0:T(8,128)(2,1)}, bf16[2,512,128]{2,1,0:T(8,128)(2,1)}, u32[]{:S(2)}, u32[]{:S(2)}) collective-permute-start(bf16[2,512,128]{2,1,0:T(8,128)(2,1)} %get-tuple-element.123), channel_id=1, source_target_pairs={{0,4},{4,8},{8,12},{12,16},{16,20},{20,24},{24,28},{1,5},{5,9},{9,... | collective-permute-start | bytes 786440 | tf_op jit(solution)/shard_map/ppermute | solution.py:19
  75.9 17.0 %collective-permute-start.1 = (bf16[2,512,128]{2,1,0:T(8,128)(2,1)}, bf16[2,512,128]{2,1,0:T(8,128)(2,1)}, u32[]{:S(2)}, u32[]{:S(2)}) collective-permute-start(bf16[2,512,128]{2,1,0:T(8,128)(2,1)} %get-tuple-element.124), channel_id=1, source_target_pairs={{4,0},{8,4},{12,8},{16,12},{20,16},{24,20},{28,24},{5,1},{9,5},{13... | collective-permute-start | bytes 786440 | tf_op jit(solution)/shard_map/ppermute | solution.py:20
  105.6 1.8 copy-start.4
  107.4 5.0 %copy-start.21 = (pred[2,4]{1,0:T(4,128)(4,1)S(1)}, pred[2,4]{1,0:T(4,128)(4,1)}, u32[]{:S(2)}) copy-start(pred[2,4]{1,0:T(4,128)(4,1)} %get-tuple-element.127) | copy-start | bytes 28
  110.3 22.4 %copy-start.11 = (bf16[128,128]{1,0:T(8,128)(2,1)S(1)}, bf16[128,128]{1,0:T(8,128)(2,1)}, u32[]{:S(2)}) copy-start(bf16[128,128]{1,0:T(8,128)(2,1)} %param.31) | copy-start | bytes 98308
  110.3 31.9 %copy-start.12 = (bf16[128,128]{1,0:T(8,128)(2,1)S(1)}, bf16[128,128]{1,0:T(8,128)(2,1)}, u32[]{:S(2)}) copy-start(bf16[128,128]{1,0:T(8,128)(2,1)} %param.32) | copy-start | bytes 98308
  110.3 41.2 %copy-start.20 = (s32[8]{0:T(128)S(1)}, s32[8]{0:T(128)}, u32[]{:S(2)}) copy-start(s32[8]{0:T(128)} %reshape.221) | copy-start | bytes 100
  112.4 99.0 %all-reduce.6.cloned.1.call-start = ((), (), s32[]{:S(2)}) async-start(), calls=%async_computation.4 | async-start | bytes 1048576 | tf_op jit(solution)/shard_map/psum | solution.py:184
  151.5 1.7 copy-start.7
  151.5 2.1 copy-start.6
  151.6 6.0 %copy-start.5 = (bf16[1024,128]{1,0:T(8,128)(2,1)S(1)}, bf16[1024,128]{1,0:T(8,128)(2,1)}, u32[]{:S(2)}) copy-start(bf16[1024,128]{1,0:T(8,128)(2,1)} %all_gather.59) | copy-start | bytes 786436
  154.0 4.1 %collective-permute-start.2 = (bf16[2,256,128]{2,1,0:T(8,128)(2,1)S(1)}, bf16[2,256,128]{2,1,0:T(8,128)(2,1)S(1)}, u32[]{:S(2)}, u32[]{:S(2)}) collective-permute-start(bf16[2,256,128]{2,1,0:T(8,128)(2,1)S(1)} %pad_maximum_fusion.4), channel_id=1, source_target_pairs={{0,4},{4,8},{8,12},{12,16},{16,20},{20,24},{24,28},{1,5},{5,9},{9,... | collective-permute-start | bytes 393224 | tf_op jit(solution)/shard_map/ppermute | solution.py:19
  156.3 3.4 collective-permute-start.3
  158.1 0.7 copy-start.10
  171.3 41.7 %all-gather.7.cloned.1.call-start = ((), (), s32[]{:S(2)}) async-start(), calls=%async_computation.5 | async-start | bytes 1179648 | tf_op jit(solution)/shard_map/all_gather | solution.py:189
  171.9 51.5 %all-gather.9.cloned.1.call-start = ((), (), s32[]{:S(2)}) async-start(), calls=%async_computation.6 | async-start | bytes 1179648 | tf_op jit(solution)/shard_map/all_gather | solution.py:192
  172.5 97.8 %all-reduce.8.cloned.1.call-start = ((), (), s32[]{:S(2)}) async-start(), calls=%async_computation.7 | async-start | bytes 1048576 | tf_op jit(solution)/shard_map/psum | solution.py:193
  212.9 14.8 %copy-start.13 = (bf16[128,128]{1,0:T(8,128)(2,1)S(1)}, bf16[128,128]{1,0:T(8,128)(2,1)}, u32[]{:S(2)}) copy-start(bf16[128,128]{1,0:T(8,128)(2,1)} %param.38) | copy-start | bytes 98308
  212.9 30.0 %copy-start.14 = (bf16[128,128]{1,0:T(8,128)(2,1)S(1)}, bf16[128,128]{1,0:T(8,128)(2,1)}, u32[]{:S(2)}) copy-start(bf16[128,128]{1,0:T(8,128)(2,1)} %param.37) | copy-start | bytes 98308
  212.9 39.3 %copy-start.15 = (bf16[128,128]{1,0:T(8,128)(2,1)S(1)}, bf16[128,128]{1,0:T(8,128)(2,1)}, u32[]{:S(2)}) copy-start(bf16[128,128]{1,0:T(8,128)(2,1)} %param.36) | copy-start | bytes 98308
  213.0 47.6 %copy-start.17 = (s32[8,3]{0,1:T(4,128)S(1)}, s32[8,3]{0,1:T(4,128)}, u32[]{:S(2)}) copy-start(s32[8,3]{0,1:T(4,128)} %param.42) | copy-start | bytes 292
  213.0 47.9 %copy-start.16 = (bf16[128,128]{1,0:T(8,128)(2,1)S(1)}, bf16[128,128]{1,0:T(8,128)(2,1)}, u32[]{:S(2)}) copy-start(bf16[128,128]{1,0:T(8,128)(2,1)} %param.35) | copy-start | bytes 98308
  213.0 57.1 %copy-start.23 = (s32[8]{0:T(128)S(1)}, s32[8]{0:T(128)}, u32[]{:S(2)}) copy-start(s32[8]{0:T(128)} %param.43) | copy-start | bytes 100
  227.7 81.9 %all-gather.11.cloned.1.call-start = ((), (), s32[]{:S(2)}) async-start(), calls=%async_computation.8 | async-start | bytes 1179648 | tf_op jit(solution)/shard_map/all_gather | solution.py:215
  270.3 6.3 %copy-start.2 = (bf16[1024,1024]{1,0:T(8,128)(2,1)S(1)}, bf16[1024,1024]{1,0:T(8,128)(2,1)}, u32[]{:S(2)}) copy-start(bf16[1024,1024]{1,0:T(8,128)(2,1)} %copy-done.1) | copy-start | bytes 6291460
  271.7 5.6 %copy-start.3 = (bf16[256,1024]{1,0:T(8,128)(2,1)}, bf16[256,1024]{1,0:T(8,128)(2,1)S(1)}, u32[]{:S(2)}) copy-start(bf16[256,1024]{1,0:T(8,128)(2,1)S(1)} %get-tuple-element.104) | copy-start | bytes 1572868
  272.8 4.5 %collective-permute-start.4 = (bf16[2,128,128]{2,1,0:T(8,128)(2,1)S(1)}, bf16[2,128,128]{2,1,0:T(8,128)(2,1)S(1)}, u32[]{:S(2)}, u32[]{:S(2)}) collective-permute-start(bf16[2,128,128]{2,1,0:T(8,128)(2,1)S(1)} %get-tuple-element.125), channel_id=1, source_target_pairs={{0,4},{4,8},{8,12},{12,16},{16,20},{20,24},{24,28},{1,5},{5,9},{9,... | collective-permute-start | bytes 196616 | tf_op jit(solution)/shard_map/ppermute | solution.py:19
  275.1 3.1 collective-permute-start.5
  286.8 2.1 copy-start.8
  289.0 0.7 copy-start.9
  293.3 2.1 copy-start.8
  295.5 0.7 copy-start.9
  296.2 13.2 %all-to-all-start = ((bf16[4,256,128]{2,1,0:T(8,128)(2,1)}), bf16[4,256,128]{2,1,0:T(8,128)(2,1)S(1)}, u32[]{:S(2)}, u32[]{:S(2)}) async-start(bf16[4,256,128]{2,1,0:T(8,128)(2,1)} %bitcast.146), calls=%async_computation | async-start | bytes 524288 | tf_op jit(solution)/shard_map/all_to_all | solution.py:213
  312.1 19.9 %all-to-all-start.1 = ((bf16[256,4,256]{2,0,1:T(8,128)(2,1)}), bf16[256,4,256]{2,0,1:T(8,128)(2,1)S(1)}, u32[]{:S(2)}, u32[]{:S(2)}) async-start(bf16[256,4,256]{2,0,1:T(8,128)(2,1)} %bitcast.110), calls=%async_computation.1 | async-start | bytes 1048576 | tf_op jit(solution)/shard_map/all_to_all | solution.py:219
Sparse Core Ops, SparseCore 0:
  10.4 57.3 all-gather.4
  112.5 35.8 all-reduce.3
  171.5 39.8 all-reduce.5
  227.8 39.4 all-reduce.7
Sparse Core Ops, SparseCore 1:
  173.7 24.5 all-gather.6
  200.0 23.3 all-gather.8
  243.0 23.3 all-gather.10
where the time goes:
time: 342 us; the launch traced here: 340 us
  blocking collectives  145 us (42%)
  waiting for transfers between devices  80.7 us (24%)
  local copies, waits for them, and re-layouts  32.6 us (10%)
  matrix products  29.8 us (9%)
  starting transfers between devices  19.9 us (6%)
  other arithmetic  16 us (5%)
  between operations  16 us (5%)
    psum x1, waiting for transfers between devices, local(): lax.psum(window_terms.astype(jnp.bfloat16), 'heads').astype(jnp.float32)  38.8 us
    all_gather x1, blocking collectives, local(): mesh_full = lax.all_gather(mesh_state, 'heads', axis=1, tiled=True)  23.2 us
    all_gather x1, blocking collectives, local(): whole_output = lax.all_gather(decoder_output, 'heads', axis=0, tiled=True)  15.2 us
    all_to_all x1, waiting for transfers between devices, local(): lax.all_to_all(updated, 'heads', split_axis=1, concat_axis=0, tiled=True)  14.3 us
    all_gather x1, blocking collectives, local(): lax.all_gather(encoder_output, 'nodes', axis=1, tiled=True)  12.1 us
    gather x6, local copies, waits for them, and re-layouts, pick_tiles(): picked = jnp.take(tile_view, chosen, axis=1)  11.5 us
    all_gather x1, blocking collectives, local(): lax.all_gather(encoder_key, 'nodes', axis=0, tiled=True)  11 us
    all_gather x1, waiting for transfers between devices, local(): lax.all_gather(shrink_weight, 'nodes', axis=1, tiled=True)  10.4 us
  transfers between devices with their start and end apart: 15, of which 7 were waited for; matrix products, arithmetic and copies ran while one was open for 9% of the time, Pallas kernels for 0%

commit v1 on v0

--- a/solution.py
+++ b/solution.py
@@ -136,7 +136,14 @@
         ),
     )
     grid_queries = (grid_query * scaling).astype(jnp.bfloat16)
-    mesh_full = lax.all_gather(mesh_state, "heads", axis=1, tiled=True)
+    ring = [mesh_state]
+    for hop in range(3):
+        ring.append(lax.ppermute(ring[-1], "heads", [(dev, (dev + 1) % 4) for dev in range(4)]))
+    mesh_full = jnp.roll(
+        jnp.concatenate(ring[::-1], axis=1),
+        (lax.axis_index("heads") + 1) * ring[0].shape[1],
+        axis=1,
+    )
     mesh_norm = normalize(mesh_full)
     (mesh_query,) = add_terms(
         mesh_norm, (mesh_blank,), (lax.all_gather(encoder_query, "nodes", axis=0, tiled=True),)

time: 342 us -> 321 us (0.939)
  blocking collectives: 145 us -> 125 us
  local copies, waits for them, and re-layouts: 32.6 us -> 25.1 us
  waiting for transfers between devices: 80.7 us -> 84.6 us
  starting transfers between devices: 19.9 us -> 23.4 us
    all_gather x1 -> x0, blocking collectives: 23.2 us -> none  [local(): mesh_full = lax.all_gather(mesh_state, 'heads', axis=1, tiled=True)]
    all_gather x1, waiting for transfers between devices: 4.94 us -> 0.49 us  [local(): grid_full = lax.all_gather(grid_state, 'heads', axis=1, tiled=True)]
    ppermute x0 -> x3, starting transfers between devices: none -> 4.35 us  [local(): lax.ppermute(ring[-1], 'heads', [(dev, (dev + 1) % 4) for dev in range(4)])]
  transfers between devices with their start and end apart: 15 -> 18, of which waited for: 7 -> 10; matrix products, arithmetic and copies ran while one was open for 9% -> 10% of each run, Pallas kernels for 0% -> 0%
where the time goes in v1:
time: 321 us; the launch traced here: 320 us
  blocking collectives  125 us (39%)
  waiting for transfers between devices  84.6 us (26%)
  matrix products  29.2 us (9%)
  local copies, waits for them, and re-layouts  25.1 us (8%)
  starting transfers between devices  23.4 us (7%)
  other arithmetic  16.4 us (5%)
  between operations  16.1 us (5%)
    psum x1, waiting for transfers between devices, local(): lax.psum(window_terms.astype(jnp.bfloat16), 'heads').astype(jnp.float32)  40.5 us
    all_gather x1, blocking collectives, local(): whole_output = lax.all_gather(decoder_output, 'heads', axis=0, tiled=True)  15.2 us
    all_to_all x1, waiting for transfers between devices, local(): lax.all_to_all(updated, 'heads', split_axis=1, concat_axis=0, tiled=True)  14.3 us
    all_gather x1, blocking collectives, local(): lax.all_gather(window_query, 'nodes', axis=0, tiled=True)  13.4 us
    all_gather x1, blocking collectives, local(): lax.all_gather(encoder_query, 'nodes', axis=0, tiled=True)  11.1 us
    all_gather x1, blocking collectives, local(): lax.all_gather(window_output, 'nodes', axis=1, tiled=True)  10.3 us
    all_gather x1, waiting for transfers between devices, local(): lax.all_gather(shrink_weight, 'nodes', axis=1, tiled=True)  10.3 us
    all_gather x1, blocking collectives, local(): lax.all_gather(encoder_output, 'nodes', axis=1, tiled=True)  10.2 us
  transfers between devices with their start and end apart: 18, of which 10 were waited for; matrix products, arithmetic and copies ran while one was open for 10% of the time, Pallas kernels for 0%

profile of v1, /device:TPU:0, one launch (start us, length us, event | category | flops | bytes accessed | tf_op | source)
XLA Modules:
  0.0 320.0 jit_solution(17755123994840812718)
XLA Ops:
  8.8 3.1 collective-permute-start
  12.7 1.3 compare_and_fusion.1
  14.7 2.9 collective-permute-done
  17.6 11.1 %all_gather.51 = bf16[1024,128]{1,0:T(8,128)(2,1)} all-gather(bf16[128,128]{1,0:T(8,128)(2,1)} %param.25), channel_id=1, replica_groups=mesh['nodes'=8,'heads'=4] {'nodes'}, dimensions={0}, use_global_device_ids=true | all-gather | bytes 294912 | tf_op jit(solution)/shard_map/all_gather | solution.py:149
  28.8 10.1 %all_gather.49 = bf16[1024,128]{1,0:T(8,128)(2,1)} all-gather(bf16[128,128]{1,0:T(8,128)(2,1)} %param.26), channel_id=1, replica_groups=mesh['nodes'=8,'heads'=4] {'nodes'}, dimensions={0}, use_global_device_ids=true | all-gather | bytes 294912 | tf_op jit(solution)/shard_map/all_gather | solution.py:133
  38.9 10.1 %all_gather.50 = bf16[1024,128]{1,0:T(8,128)(2,1)} all-gather(bf16[128,128]{1,0:T(8,128)(2,1)} %param.27), channel_id=1, replica_groups=mesh['nodes'=8,'heads'=4] {'nodes'}, dimensions={0}, use_global_device_ids=true | all-gather | bytes 294912 | tf_op jit(solution)/shard_map/all_gather | solution.py:134
  49.0 1.2 collective-permute-start.2
  50.2 10.2 %all_gather.52 = bf16[128,1024]{1,0:T(8,128)(2,1)} all-gather(bf16[128,128]{1,0:T(8,128)(2,1)} %param.28), channel_id=1, replica_groups=mesh['nodes'=8,'heads'=4] {'nodes'}, dimensions={1}, use_global_device_ids=true | all-gather | bytes 294912 | tf_op jit(solution)/shard_map/all_gather | solution.py:162
  62.2 2.1 convert_reduce_fusion
  68.8 2.5 collective-permute-start.3
  71.3 1.3 collective-permute-start.4
  72.6 1.0 fusion.26
  73.6 0.9 reshape.241
  74.6 1.0 collective-permute-done.4
  75.6 1.2 pad_maximum_fusion
  76.8 1.7 gather_fusion
  78.4 1.7 copy.50
  80.4 1.0 reshape.205
  81.4 1.0 reshape.203
  82.4 1.8 fusion.173
  84.2 2.2 fusion.28
  86.6 1.1 convolution_convert_fusion.3
  87.9 13.4 %all_gather.55 = bf16[1024,128]{1,0:T(8,128)(2,1)S(1)} all-gather(bf16[128,128]{1,0:T(8,128)(2,1)S(1)} %copy-done.16), channel_id=1, replica_groups=mesh['nodes'=8,'heads'=4] {'nodes'}, dimensions={0}, use_global_device_ids=true | all-gather | bytes 294912 | tf_op jit(solution)/shard_map/all_gather | solution.py:171
  101.3 9.2 %all_gather.53 = bf16[1024,128]{1,0:T(8,128)(2,1)S(1)} all-gather(bf16[128,128]{1,0:T(8,128)(2,1)S(1)} %copy-done.17), channel_id=1, replica_groups=mesh['nodes'=8,'heads'=4] {'nodes'}, dimensions={0}, use_global_device_ids=true | all-gather | bytes 294912 | tf_op jit(solution)/shard_map/all_gather | solution.py:172
  110.5 8.5 %all_gather.54 = bf16[1024,128]{1,0:T(8,128)(2,1)S(1)} all-gather(bf16[128,128]{1,0:T(8,128)(2,1)S(1)} %copy-done.18), channel_id=1, replica_groups=mesh['nodes'=8,'heads'=4] {'nodes'}, dimensions={0}, use_global_device_ids=true | all-gather | bytes 294912 | tf_op jit(solution)/shard_map/all_gather | solution.py:173
  119.0 10.3 %all_gather.56 = bf16[128,1024]{1,0:T(8,128)(2,1)} all-gather(bf16[128,128]{1,0:T(8,128)(2,1)S(1)} %copy-done.19), channel_id=1, replica_groups=mesh['nodes'=8,'heads'=4] {'nodes'}, dimensions={1}, use_global_device_ids=true | all-gather | bytes 294912 | tf_op jit(solution)/shard_map/all_gather | solution.py:189
  129.3 1.1 all-reduce.4.cloned.1.call-done
  130.4 1.4 convert_reduce_fusion.2
  132.9 1.3 collective-permute-start.5
  134.2 1.3 collective-permute-start.6
  136.7 2.6 collective-permute-done.6
  139.3 0.9 pad_maximum_fusion.1
  140.9 1.1 copy.54
  142.0 1.4 select_bitcast_fusion.2
  143.6 1.2 convolution_select_fusion.1
  145.5 2.7 fusion.31
  148.2 1.1 convolution_convert_fusion.2
  150.6 40.5 %all-reduce.6.cloned.1.call-done = bf16[256,1024]{1,0:T(8,128)(2,1)} async-done(((bf16[256,1024]{1,0:T(8,128)(2,1)}), bf16[256,1024]{1,0:T(8,128)(2,1)}) %all-reduce.6.cloned.1.call-update) | async-done | bytes 524304 | tf_op jit(solution)/shard_map/psum | solution.py:191
  191.1 1.3 convert_reduce_fusion.1
  192.8 10.3 %all-gather.9.cloned.1.call-done = bf16[512,1024]{1,0:T(8,128)(2,1)} async-done(((bf16[512,128]{1,0:T(8,128)(2,1)}), bf16[512,1024]{1,0:T(8,128)(2,1)}) %all-gather.9.cloned.1.call-update) | async-done | bytes 1048592 | tf_op jit(solution)/shard_map/all_gather | solution.py:199
  203.1 4.3 %convolution_convert_fusion.1 = bf16[256,1024]{1,0:T(8,128)(2,1)} fusion(bf16[512,1024]{1,0:T(8,128)(2,1)} %all-gather.9.cloned.1.call-done, bf16[1024,512]{1,0:T(8,128)(2,1)} %all-gather.7.cloned.1.call-done, bf16[256,1024]{1,0:T(8,128)(2,1)S(1)} %get-tuple-element.106, f32[256]{0:T(256)S(1)} %add_rsqrt_fusion.2, f32[256]{0:T(256)S(1)} %broadcast_multiply_fusion.2), kind=kOutput, calls=%fused_computation.44 | convolution fusion | flops 546701312 | bytes 3147776 | tf_op jit(solution)/shard_map/dot_general | solution.py:41
  207.4 15.2 %all_gather.62 = bf16[512,128]{1,0:T(8,128)(2,1)} all-gather(bf16[128,128]{1,0:T(8,128)(2,1)S(1)} %copy-done.20), channel_id=1, replica_groups=mesh['nodes'=8,'heads'=4] {'heads'}, dimensions={0}, use_global_device_ids=true | all-gather | bytes 163840 | tf_op jit(solution)/shard_map/all_gather | solution.py:221
  222.6 9.3 %all_gather.60 = bf16[1024,128]{1,0:T(8,128)(2,1)S(1)} all-gather(bf16[128,128]{1,0:T(8,128)(2,1)S(1)} %copy-done.21), channel_id=1, replica_groups=mesh['nodes'=8,'heads'=4] {'nodes'}, dimensions={0}, use_global_device_ids=true | all-gather | bytes 294912 | tf_op jit(solution)/shard_map/all_gather | solution.py:209
  231.9 8.3 %all_gather.59 = bf16[1024,128]{1,0:T(8,128)(2,1)S(1)} all-gather(bf16[128,128]{1,0:T(8,128)(2,1)S(1)} %copy-done.22), channel_id=1, replica_groups=mesh['nodes'=8,'heads'=4] {'nodes'}, dimensions={0}, use_global_device_ids=true | all-gather | bytes 294912 | tf_op jit(solution)/shard_map/all_gather | solution.py:208
  240.5 9.3 %all_gather.61 = bf16[1024,128]{1,0:T(8,128)(2,1)S(1)} all-gather(bf16[128,128]{1,0:T(8,128)(2,1)S(1)} %copy-done.23), channel_id=1, replica_groups=mesh['nodes'=8,'heads'=4] {'nodes'}, dimensions={0}, use_global_device_ids=true | all-gather | bytes 294912 | tf_op jit(solution)/shard_map/all_gather | solution.py:135
  250.0 1.4 convert_reduce_fusion.4
  252.5 2.3 collective-permute-start.7
  254.8 1.5 collective-permute-start.8
  257.9 2.0 gather_fusion.2
  259.9 1.5 copy.59
  261.6 1.3 fusion.170
  262.9 13.1 %while.2 = (s32[]{:T(128)}, bf16[2,4,128,128]{3,2,1,0:T(8,128)(2,1)}, bf16[2,4,384,128]{3,2,1,0:T(8,128)(2,1)}, pred[2,4,384]{2,1,0:T(4,128)(4,1)S(1)}, bf16[2,4...) while((s32[]{:T(128)}, bf16[2,4,128,128]{3,2,1,0:T(8,128)(2,1)}, ...), condition=%wide.region_20.21_spmd, body=%wide.region_17.20_spmd.sunk | while | flops 102695296 | bytes 10498709 | solution.py:76
  262.9 1.2 constant_dynamic-slice_fusion.6
  264.5 1.8 fusion.214
  266.5 2.0 convolution_convert_fusion.13
  269.4 1.2 constant_dynamic-slice_fusion.6
  271.0 1.8 fusion.214
  273.1 2.0 convolution_convert_fusion.13
  276.0 4.6 %all-to-all-start = ((bf16[4,256,128]{2,1,0:T(8,128)(2,1)}), bf16[4,256,128]{2,1,0:T(8,128)(2,1)S(1)}, u32[]{:S(2)}, u32[]{:S(2)}) async-start(bf16[4,256,128]{2,1,0:T(8,128)(2,1)} %bitcast.146), calls=%async_computation | async-start | bytes 524288 | tf_op jit(solution)/shard_map/all_to_all | solution.py:220
  280.6 8.6 %all-to-all-done = bf16[4,256,128]{2,1,0:T(8,128)(2,1)S(1)} async-done(((bf16[4,256,128]{2,1,0:T(8,128)(2,1)}), bf16[4,256,128]{2,1,0:T(8,128)(2,1)S(1)}, u32[]{:S(2)}, u32[]{:S(2)}) %all-to-all-start) | async-done | bytes 262176 | tf_op jit(solution)/shard_map/all_to_all | solution.py:220
  289.4 1.7 fusion.14
  291.9 4.1 %all-to-all-start.1 = ((bf16[256,4,256]{2,0,1:T(8,128)(2,1)}), bf16[256,4,256]{2,0,1:T(8,128)(2,1)S(1)}, u32[]{:S(2)}, u32[]{:S(2)}) async-start(bf16[256,4,256]{2,0,1:T(8,128)(2,1)} %bitcast.110), calls=%async_computation.1 | async-start | bytes 1048576 | tf_op jit(solution)/shard_map/all_to_all | solution.py:226
  296.0 1.6 constant_dynamic-slice_fusion.3
  297.5 14.3 %all-to-all-done.1 = bf16[256,4,256]{2,0,1:T(8,128)(2,1)S(1)} async-done(((bf16[256,4,256]{2,0,1:T(8,128)(2,1)}), bf16[256,4,256]{2,0,1:T(8,128)(2,1)S(1)}, u32[]{:S(2)}, u32[]{:S(2)}) %all-to-all-start.1) | async-done | bytes 524320 | tf_op jit(solution)/shard_map/all_to_all | solution.py:226
  (170 shorter events, 22.4 us)
Async XLA Ops:
  8.0 53.2 %copy-start.11 = (bf16[256,256]{1,0:T(8,128)(2,1)S(1)}, bf16[256,256]{1,0:T(8,128)(2,1)}, u32[]{:S(2)}) copy-start(bf16[256,256]{1,0:T(8,128)(2,1)} %param.24) | copy-start | bytes 393220
  8.0 54.2 %all-gather.5.cloned.1.call-start = ((), (), s32[]{:S(2)}) async-start(), calls=%async_computation.2 | async-start | bytes 2621440 | tf_op jit(solution)/shard_map/all_gather | solution.py:127
  8.7 121.7 %all-reduce.4.cloned.1.call-start = ((), (), s32[]{:S(2)}) async-start(), calls=%async_computation.3 | async-start | bytes 1048576 | tf_op jit(solution)/shard_map/psum | solution.py:164
  8.8 8.8 %collective-permute-start = (bf16[256,256]{1,0:T(8,128)(2,1)}, bf16[256,256]{1,0:T(8,128)(2,1)S(1)}, u32[]{:S(2)}, u32[]{:S(2)}) collective-permute-start(bf16[256,256]{1,0:T(8,128)(2,1)} %param.24), channel_id=1, source_target_pairs={{0,1},{1,2},{2,3},{3,0},{4,5},{5,6},{6,7},{7,4},{8,9},{9,10},{10,1... | collective-permute-start | bytes 393224 | tf_op jit(solution)/shard_map/ppermute | solution.py:141
  17.6 31.4 %collective-permute-start.1 = (bf16[256,256]{1,0:T(8,128)(2,1)S(1)}, bf16[256,256]{1,0:T(8,128)(2,1)S(1)}, u32[]{:S(2)}, u32[]{:S(2)}) collective-permute-start(bf16[256,256]{1,0:T(8,128)(2,1)S(1)} %collective-permute-done), channel_id=1, source_target_pairs={{0,1},{1,2},{2,3},{3,0},{4,5},{5,6},{6,7},{7,4},{8,9},{9,10},{10,1... | collective-permute-start | bytes 393224 | tf_op jit(solution)/shard_map/ppermute | solution.py:141
  49.0 12.1 %collective-permute-start.2 = (bf16[256,256]{1,0:T(8,128)(2,1)S(1)}, bf16[256,256]{1,0:T(8,128)(2,1)S(1)}, u32[]{:S(2)}, u32[]{:S(2)}) collective-permute-start(bf16[256,256]{1,0:T(8,128)(2,1)S(1)} %collective-permute-done.1), channel_id=1, source_target_pairs={{0,1},{1,2},{2,3},{3,0},{4,5},{5,6},{6,7},{7,4},{8,9},{9,10},{10,1... | collective-permute-start | bytes 393224 | tf_op jit(solution)/shard_map/ppermute | solution.py:141
  61.3 11.4 %copy-start.3 = (bf16[256,2048]{1,0:T(8,128)(2,1)}, bf16[256,2048]{1,0:T(8,128)(2,1)S(1)}, u32[]{:S(2)}) copy-start(bf16[256,2048]{1,0:T(8,128)(2,1)S(1)} %constant_dynamic-update-slice_fusion.1) | copy-start | bytes 3145732
  62.2 2.2 copy-start
  65.1 1.0 copy-start.7
  66.1 1.8 copy-start.1
  66.1 1.1 copy-start.6
  67.2 5.4 %copy-start.13 = (bf16[1024,128]{1,0:T(8,128)(2,1)S(1)}, bf16[1024,128]{1,0:T(8,128)(2,1)}, u32[]{:S(2)}) copy-start(bf16[1024,128]{1,0:T(8,128)(2,1)} %all_gather.51) | copy-start | bytes 786436
  67.9 0.9 copy-start.5
  68.8 5.8 %collective-permute-start.3 = (bf16[2,512,128]{2,1,0:T(8,128)(2,1)}, bf16[2,512,128]{2,1,0:T(8,128)(2,1)}, u32[]{:S(2)}, u32[]{:S(2)}) collective-permute-start(bf16[2,512,128]{2,1,0:T(8,128)(2,1)} %get-tuple-element.123), channel_id=1, source_target_pairs={{0,4},{4,8},{8,12},{12,16},{16,20},{20,24},{24,28},{1,5},{5,9},{9,... | collective-permute-start | bytes 786440 | tf_op jit(solution)/shard_map/ppermute | solution.py:19
  71.3 4.3 %collective-permute-start.4 = (bf16[2,512,128]{2,1,0:T(8,128)(2,1)}, bf16[2,512,128]{2,1,0:T(8,128)(2,1)}, u32[]{:S(2)}, u32[]{:S(2)}) collective-permute-start(bf16[2,512,128]{2,1,0:T(8,128)(2,1)} %get-tuple-element.124), channel_id=1, source_target_pairs={{4,0},{8,4},{12,8},{16,12},{20,16},{24,20},{28,24},{5,1},{9,5},{13... | collective-permute-start | bytes 786440 | tf_op jit(solution)/shard_map/ppermute | solution.py:20
  81.4 2.8 copy-start.10
  84.2 2.4 copy-start.8
  84.2 3.6 %copy-start.26 = (pred[2,4]{1,0:T(4,128)(4,1)S(1)}, pred[2,4]{1,0:T(4,128)(4,1)}, u32[]{:S(2)}) copy-start(pred[2,4]{1,0:T(4,128)(4,1)} %get-tuple-element.127) | copy-start | bytes 28
  84.2 3.7 %copy-start.16 = (bf16[128,128]{1,0:T(8,128)(2,1)S(1)}, bf16[128,128]{1,0:T(8,128)(2,1)}, u32[]{:S(2)}) copy-start(bf16[128,128]{1,0:T(8,128)(2,1)} %param.29) | copy-start | bytes 98308
  84.2 17.1 %copy-start.17 = (bf16[128,128]{1,0:T(8,128)(2,1)S(1)}, bf16[128,128]{1,0:T(8,128)(2,1)}, u32[]{:S(2)}) copy-start(bf16[128,128]{1,0:T(8,128)(2,1)} %param.30) | copy-start | bytes 98308
  86.5 24.1 %copy-start.18 = (bf16[128,128]{1,0:T(8,128)(2,1)S(1)}, bf16[128,128]{1,0:T(8,128)(2,1)}, u32[]{:S(2)}) copy-start(bf16[128,128]{1,0:T(8,128)(2,1)} %param.31) | copy-start | bytes 98308
  86.5 32.6 %copy-start.19 = (bf16[128,128]{1,0:T(8,128)(2,1)S(1)}, bf16[128,128]{1,0:T(8,128)(2,1)}, u32[]{:S(2)}) copy-start(bf16[128,128]{1,0:T(8,128)(2,1)} %param.32) | copy-start | bytes 98308
  86.5 42.8 %copy-start.25 = (s32[8]{0:T(128)S(1)}, s32[8]{0:T(128)}, u32[]{:S(2)}) copy-start(s32[8]{0:T(128)} %reshape.221) | copy-start | bytes 100
  87.7 103.4 %all-reduce.6.cloned.1.call-start = ((), (), s32[]{:S(2)}) async-start(), calls=%async_computation.4 | async-start | bytes 1048576 | tf_op jit(solution)/shard_map/psum | solution.py:191
  132.9 3.8 %collective-permute-start.5 = (bf16[2,256,128]{2,1,0:T(8,128)(2,1)S(1)}, bf16[2,256,128]{2,1,0:T(8,128)(2,1)S(1)}, u32[]{:S(2)}, u32[]{:S(2)}) collective-permute-start(bf16[2,256,128]{2,1,0:T(8,128)(2,1)S(1)} %pad_maximum_fusion.4), channel_id=1, source_target_pairs={{0,4},{4,8},{8,12},{12,16},{16,20},{20,24},{24,28},{1,5},{5,9},{9,... | collective-permute-start | bytes 393224 | tf_op jit(solution)/shard_map/ppermute | solution.py:19
  134.2 5.1 %collective-permute-start.6 = (bf16[2,256,128]{2,1,0:T(8,128)(2,1)S(1)}, bf16[2,256,128]{2,1,0:T(8,128)(2,1)}, u32[]{:S(2)}, u32[]{:S(2)}) collective-permute-start(bf16[2,256,128]{2,1,0:T(8,128)(2,1)S(1)} %pad_maximum_fusion.4), channel_id=1, source_target_pairs={{4,0},{8,4},{12,8},{16,12},{20,16},{24,20},{28,24},{5,1},{9,5},{13... | collective-permute-start | bytes 393224 | tf_op jit(solution)/shard_map/ppermute | solution.py:20
  142.0 1.7 copy-start.12
  145.5 2.7 copy-start.9
  149.4 43.4 %all-gather.7.cloned.1.call-start = ((), (), s32[]{:S(2)}) async-start(), calls=%async_computation.5 | async-start | bytes 1179648 | tf_op jit(solution)/shard_map/all_gather | solution.py:196
  149.9 53.1 %all-gather.9.cloned.1.call-start = ((), (), s32[]{:S(2)}) async-start(), calls=%async_computation.6 | async-start | bytes 1179648 | tf_op jit(solution)/shard_map/all_gather | solution.py:199
  150.5 99.4 %all-reduce.8.cloned.1.call-start = ((), (), s32[]{:S(2)}) async-start(), calls=%async_computation.7 | async-start | bytes 1048576 | tf_op jit(solution)/shard_map/psum | solution.py:200
  192.7 14.7 %copy-start.20 = (bf16[128,128]{1,0:T(8,128)(2,1)S(1)}, bf16[128,128]{1,0:T(8,128)(2,1)}, u32[]{:S(2)}) copy-start(bf16[128,128]{1,0:T(8,128)(2,1)} %param.38) | copy-start | bytes 98308
  192.7 29.9 %copy-start.21 = (bf16[128,128]{1,0:T(8,128)(2,1)S(1)}, bf16[128,128]{1,0:T(8,128)(2,1)}, u32[]{:S(2)}) copy-start(bf16[128,128]{1,0:T(8,128)(2,1)} %param.37) | copy-start | bytes 98308
  192.7 39.2 %copy-start.22 = (bf16[128,128]{1,0:T(8,128)(2,1)S(1)}, bf16[128,128]{1,0:T(8,128)(2,1)}, u32[]{:S(2)}) copy-start(bf16[128,128]{1,0:T(8,128)(2,1)} %param.36) | copy-start | bytes 98308
  192.7 47.5 %copy-start.24 = (s32[8,3]{0,1:T(4,128)S(1)}, s32[8,3]{0,1:T(4,128)}, u32[]{:S(2)}) copy-start(s32[8,3]{0,1:T(4,128)} %param.42) | copy-start | bytes 292
  192.8 47.8 %copy-start.23 = (bf16[128,128]{1,0:T(8,128)(2,1)S(1)}, bf16[128,128]{1,0:T(8,128)(2,1)}, u32[]{:S(2)}) copy-start(bf16[128,128]{1,0:T(8,128)(2,1)} %param.35) | copy-start | bytes 98308
  192.8 57.0 %copy-start.27 = (s32[8]{0:T(128)S(1)}, s32[8]{0:T(128)}, u32[]{:S(2)}) copy-start(s32[8]{0:T(128)} %param.43) | copy-start | bytes 100
  207.4 82.0 %all-gather.11.cloned.1.call-start = ((), (), s32[]{:S(2)}) async-start(), calls=%async_computation.8 | async-start | bytes 1179648 | tf_op jit(solution)/shard_map/all_gather | solution.py:222
  250.0 6.3 %copy-start.2 = (bf16[1024,1024]{1,0:T(8,128)(2,1)S(1)}, bf16[1024,1024]{1,0:T(8,128)(2,1)}, u32[]{:S(2)}) copy-start(bf16[1024,1024]{1,0:T(8,128)(2,1)} %copy-done.1) | copy-start | bytes 6291460
  251.4 5.6 %copy-start.4 = (bf16[256,1024]{1,0:T(8,128)(2,1)}, bf16[256,1024]{1,0:T(8,128)(2,1)S(1)}, u32[]{:S(2)}) copy-start(bf16[256,1024]{1,0:T(8,128)(2,1)S(1)} %get-tuple-element.104) | copy-start | bytes 1572868
  252.5 4.5 %collective-permute-start.7 = (bf16[2,128,128]{2,1,0:T(8,128)(2,1)S(1)}, bf16[2,128,128]{2,1,0:T(8,128)(2,1)S(1)}, u32[]{:S(2)}, u32[]{:S(2)}) collective-permute-start(bf16[2,128,128]{2,1,0:T(8,128)(2,1)S(1)} %get-tuple-element.125), channel_id=1, source_target_pairs={{0,4},{4,8},{8,12},{12,16},{16,20},{20,24},{24,28},{1,5},{5,9},{9,... | collective-permute-start | bytes 196616 | tf_op jit(solution)/shard_map/ppermute | solution.py:19
  254.8 3.1 collective-permute-start.8
  266.5 2.1 copy-start.14
  268.7 0.7 copy-start.15
  273.1 2.1 copy-start.14
  275.2 0.7 copy-start.15
  276.0 13.2 %all-to-all-start = ((bf16[4,256,128]{2,1,0:T(8,128)(2,1)}), bf16[4,256,128]{2,1,0:T(8,128)(2,1)S(1)}, u32[]{:S(2)}, u32[]{:S(2)}) async-start(bf16[4,256,128]{2,1,0:T(8,128)(2,1)} %bitcast.146), calls=%async_computation | async-start | bytes 524288 | tf_op jit(solution)/shard_map/all_to_all | solution.py:220
  291.9 19.9 %all-to-all-start.1 = ((bf16[256,4,256]{2,0,1:T(8,128)(2,1)}), bf16[256,4,256]{2,0,1:T(8,128)(2,1)S(1)}, u32[]{:S(2)}, u32[]{:S(2)}) async-start(bf16[256,4,256]{2,0,1:T(8,128)(2,1)} %bitcast.110), calls=%async_computation.1 | async-start | bytes 1048576 | tf_op jit(solution)/shard_map/all_to_all | solution.py:226
Sparse Core Ops, SparseCore 0:
  10.4 51.7 all-gather.4
  87.9 42.5 all-reduce.3
  149.5 41.5 all-reduce.5
  207.5 39.4 all-reduce.7
Sparse Core Ops, SparseCore 1:
  151.7 26.1 all-gather.6
  179.7 23.3 all-gather.8
  222.7 23.3 all-gather.10
